TPU v7x, 128 devices: a whole 4x4x4 slice. The times are simulated.
128 devices in a mesh: side: 2 (over core), shard: 64 (over y, x, z).
Axes of the slice: x: 4, y: 4, z: 4, core: 2. Of those that a mesh axis runs over, the one named last changes fastest.
Arguments:
- sketch: bfloat16 [2, 131072, 128], P('side', 'shard'), may hold values from -6 to 6
- tile_values: bfloat16 [2, 327680, 1024], P('side', 'shard'), may hold values from -100 to 100, as said below
- sent_blocks: int32 [2, 2560], P(None, 'shard'), may hold values from 0 to 15, as said below
- pair_counts: int32 [2, 320], P(None, 'shard'), may hold values from 4 to 8, as said below
Outputs:
- new_sketch: float32 [2, 131072, 128], P('side', 'shard')
Inputs may be any that keep to these rules, and one draw needn't show every extreme that they name: The two sides hold one matrix: tile_values[1, o, j] is the transpose of tile_values[0, (o + j - 2) mod 64, 4 - j] in the layout of the first step. `sent_blocks`: the 8 entries of one side, owner and pair are distinct. `pair_counts`: for every side and owner some pair uses all 8 slots.
All inputs are finite; a program needn't handle non-finite values.
Results may differ from a plain program's by a relative error of at most 0.0003.
Values may be sent and summed in bfloat16 or wider, within the bound.
A program may use at most 64 MiB of HBM per device.

v0:
```python
import jax
import jax.numpy as jnp
from jax import lax
from jax.sharding import PartitionSpec as P

TB = 128
RANK = 128
PEER = 8
HALF = 2
PAIRS = 5
EPSILON = 1e-05


def from_partner(block, axis, stride):
    count = lax.axis_size(axis)
    route = []
    for low in range(count):
        high = low | 1 << stride
        if high != low and high < count:
            route += [(low, high), (high, low)]
    return lax.ppermute(block, axis, route)


def from_behind(x, axis, by):
    length = lax.axis_size(axis)
    return lax.ppermute(x, axis, [(i, (i + by) % length) for i in range(length)])


def select_rows(stacked, position):
    return lax.dynamic_index_in_dim(stacked, position, 0, keepdims=False)


def packed_blocks(source, chosen, live_count):
    picked = source[chosen]
    places = jnp.arange(chosen.shape[1], dtype=jnp.int32)
    usable = places[None, :] < live_count[:, None]
    return jnp.where(usable[:, :, None, None], picked, jnp.zeros_like(picked))


def body(sketch, tile_values, sent_blocks, pair_counts):
    side_pos = lax.axis_index("side")
    block_rows = sketch.shape[1] // TB
    own_sketch = sketch[0].reshape(block_rows, TB, RANK)
    block_lists = sent_blocks.reshape(2, PAIRS, PEER)
    own_lists = select_rows(block_lists, side_pos)
    far_lists = select_rows(block_lists, 1 - side_pos)
    own_counts = select_rows(pair_counts, side_pos)
    far_counts = select_rows(pair_counts, 1 - side_pos)
    facing = from_partner(own_sketch, "side", 0)
    crossed = packed_blocks(facing, far_lists, far_counts)
    offsets = [pair_pos - HALF for pair_pos in range(PAIRS)]
    arrived = [crossed[HALF]] * PAIRS
    for pair_pos in range(PAIRS):
        if offsets[pair_pos] != 0:
            arrived[pair_pos] = from_behind(crossed[pair_pos], "shard", offsets[pair_pos])
    fetched = jnp.stack(arrived[::-1]).reshape(PAIRS, PEER * TB, RANK)
    tile_grid = tile_values[0].reshape(PAIRS, PEER * TB, PEER * TB)
    product = jnp.einsum("jab,jbr->jar", tile_grid, fetched, preferred_element_type=jnp.float32)
    places = jnp.arange(PEER, dtype=jnp.int32)
    usable = places[None, :] < own_counts[:, None]
    targets = jnp.arange(block_rows, dtype=jnp.int32)
    routing = ((own_lists[:, :, None] == targets[None, None, :]) & usable[:, :, None]).astype(
        jnp.float32
    )
    update = jnp.einsum(
        "jak,jatr->ktr",
        routing,
        product.reshape(PAIRS, PEER, TB, RANK),
        precision=lax.Precision.HIGHEST,
    ).reshape(block_rows * TB, RANK)
    partial_value = jnp.einsum("nr,ns->rs", update, update, precision=lax.Precision.HIGHEST)
    summed = lax.psum(partial_value, "shard")
    owners = lax.axis_size("shard")
    gram_matrix = summed / (update.shape[0] * owners) + EPSILON * jnp.eye(RANK, dtype=jnp.float32)
    factor = jnp.linalg.cholesky(gram_matrix)
    result = jax.scipy.linalg.solve_triangular(factor, update.T, lower=True).T
    return result[None]


def solution(mesh):
    return jax.shard_map(
        body,
        mesh=mesh,
        in_specs=(
            P("side", "shard", None),
            P("side", "shard", None),
            P(None, "shard"),
            P(None, "shard"),
        ),
        out_specs=P("side", "shard", None),
        check_vma=False,
    )
```

profile of v0, /device:TPU:0, one launch (start us, length us, event | category | flops | bytes accessed | tf_op | source)
XLA Modules:
  0.0 211.4 jit_solution(3255072321141772111)
XLA Ops:
  6.5 0.8 reshape.109
  7.4 0.8 fusion.9
  8.7 0.8 gather_fusion
  9.8 4.1 %collective-permute-start.1 = (bf16[8,128,128]{2,1,0:T(8,128)(2,1)S(1)}, bf16[8,128,128]{2,1,0:T(8,128)(2,1)S(1)}, u32[]{:S(2)}, u32[]{:S(2)}) collective-permute-start(bf16[8,128,128]{2,1,0:T(8,128)(2,1)S(1)} %get-tuple-element.9), channel_id=1, source_target_pairs={{0,2},{1,3},{2,4},{3,5},{4,6},{5,7},{6,8},{7,9},{8,10},{9,11},{10,... | collective-permute-start | bytes 786440 | tf_op jit(solution)/shard_map/ppermute | solution.py:26
  13.8 1.0 collective-permute-start.2
  14.8 6.4 %collective-permute-start.3 = (bf16[8,128,128]{2,1,0:T(8,128)(2,1)S(1)}, bf16[8,128,128]{2,1,0:T(8,128)(2,1)S(1)}, u32[]{:S(2)}, u32[]{:S(2)}) collective-permute-start(bf16[8,128,128]{2,1,0:T(8,128)(2,1)S(1)} %get-tuple-element.6), channel_id=1, source_target_pairs={{0,63},{1,0},{2,1},{3,2},{4,3},{5,4},{6,5},{7,6},{8,7},{9,8},{10,9... | collective-permute-start | bytes 786440 | tf_op jit(solution)/shard_map/ppermute | solution.py:26
  21.8 3.7 %collective-permute-done.1 = bf16[8,128,128]{2,1,0:T(8,128)(2,1)S(1)} collective-permute-done((bf16[8,128,128]{2,1,0:T(8,128)(2,1)S(1)}, bf16[8,128,128]{2,1,0:T(8,128)(2,1)S(1)}, u32[]{:S(2)}, u32[]{:S(2)}) %collective-permute-start.1) | collective-permute-done | bytes 262176 | tf_op jit(solution)/shard_map/ppermute | solution.py:26
  25.6 7.2 %collective-permute-done.2 = bf16[8,128,128]{2,1,0:T(8,128)(2,1)S(1)} collective-permute-done((bf16[8,128,128]{2,1,0:T(8,128)(2,1)S(1)}, bf16[8,128,128]{2,1,0:T(8,128)(2,1)S(1)}, u32[]{:S(2)}, u32[]{:S(2)}) %collective-permute-start.2) | collective-permute-done | bytes 262176 | tf_op jit(solution)/shard_map/ppermute | solution.py:26
  32.9 4.0 %collective-permute-done.3 = bf16[8,128,128]{2,1,0:T(8,128)(2,1)S(1)} collective-permute-done((bf16[8,128,128]{2,1,0:T(8,128)(2,1)S(1)}, bf16[8,128,128]{2,1,0:T(8,128)(2,1)S(1)}, u32[]{:S(2)}, u32[]{:S(2)}) %collective-permute-start.3) | collective-permute-done | bytes 262176 | tf_op jit(solution)/shard_map/ppermute | solution.py:26
  37.3 7.6 %fusion.11 = f32[5,128,1024]{2,1,0:T(8,128)S(1)} fusion(bf16[5,1024,128]{1,2,0:T(8,128)(2,1)S(1)} %constant_dynamic-update-slice_fusion, bf16[5,1024,1024]{2,1,0:T(8,128)(2,1)} %bitcast.55), kind=kOutput, calls=%fused_computation.40 | convolution fusion | flops 1342177280 | bytes 14417920 | tf_op jit(solution)/shard_map/jab,jbr->jar/dot_general | solution.py:58
  44.9 2.1 %copy.27 = f32[80,8,8,128]{3,2,1,0:T(8,128)} copy(f32[80,8,8,128]{3,1,2,0:T(8,128)S(1)} %bitcast.56) | data formatting | bytes 5242880
  47.1 2.6 %copy.14 = f32[5,8,128,128]{3,1,0,2:T(8,128)S(1)} copy(f32[5,8,128,128]{2,1,3,0:T(8,128)} %bitcast.57) | data formatting | bytes 5242880 | tf_op jit(solution)/shard_map/reshape | solution.py:68
  49.6 1.1 convolution_bitcast_fusion.1
  50.7 1.0 copy-done
  51.7 2.5 %convolution_bitcast_fusion.2 = f32[128,128]{1,0:T(8,128)} fusion(f32[16,128,128]{2,0,1:T(8,128)S(1)} %convolution_bitcast_fusion.1), kind=kOutput, calls=%fused_computation.4 | convolution fusion | flops 402653184 | bytes 1114112 | tf_op jit(solution)/shard_map/nr,ns->rs/dot_general | solution.py:71
  54.2 1.6 copy.15
  55.8 122.2 %all-reduce.2.cloned.1.call-done = f32[128,128]{1,0:T(8,128)} async-done(((f32[128,128]{1,0:T(8,128)}), f32[128,128]{1,0:T(8,128)}) %all-reduce.2.cloned.1.call-update) | async-done | bytes 65552 | tf_op jit(solution)/shard_map/psum | solution.py:72
  178.0 0.9 select_add_fusion
  178.9 0.9 fusion.2
  179.8 11.7 %cholesky.16 = f32[128,128]{1,0:T(8,128)S(1)} custom-call(f32[128,128]{1,0:T(8,128)S(1)} %fusion.2), custom_call_target="Cholesky" | custom-call | tf_op jit(solution)/shard_map/jit(cholesky)/cholesky | solution.py:75
  191.5 0.6 compare_reduce_fusion
  192.2 0.7 fusion
  192.8 9.8 %custom-call.7 = f32[1,128,128]{1,2,0:T(8,128)S(1)} custom-call(f32[1,128,128]{2,1,0:T(8,128)S(1)} %fusion), custom_call_target="InvertDiagBlocksLowerTriangular" | custom-call | tf_op jit(solution)/shard_map/jit(_solve_triangular)/triangular_solve | solution.py:76
  202.7 1.9 convolution_bitcast_fusion
  (27 shorter events, 2.2 us)
Async XLA Ops:
  6.5 171.4 %all-reduce.2.cloned.1.call-start = ((), (), s32[]{:S(2)}) async-start(), calls=%async_computation | async-start | bytes 131072 | tf_op jit(solution)/shard_map/psum | solution.py:72
  6.5 2.1 %collective-permute-start = (bf16[16,128,128]{2,1,0:T(8,128)(2,1)}, bf16[16,128,128]{2,1,0:T(8,128)(2,1)S(1)}, u32[]{:S(2)}, u32[]{:S(2)}) collective-permute-start(bf16[16,128,128]{2,1,0:T(8,128)(2,1)} %bitcast.65), channel_id=1, source_target_pairs={{0,64},{64,0},{1,65},{65,1},{2,66},{66,2},{3,67},{67,3},{4,68},{68... | collective-permute-start | bytes 1572872 | tf_op jit(solution)/shard_map/ppermute | solution.py:21
  9.8 15.7 %collective-permute-start.1 = (bf16[8,128,128]{2,1,0:T(8,128)(2,1)S(1)}, bf16[8,128,128]{2,1,0:T(8,128)(2,1)S(1)}, u32[]{:S(2)}, u32[]{:S(2)}) collective-permute-start(bf16[8,128,128]{2,1,0:T(8,128)(2,1)S(1)} %get-tuple-element.9), channel_id=1, source_target_pairs={{0,2},{1,3},{2,4},{3,5},{4,6},{5,7},{6,8},{7,9},{8,10},{9,11},{10,... | collective-permute-start | bytes 786440 | tf_op jit(solution)/shard_map/ppermute | solution.py:26
  13.8 19.0 %collective-permute-start.2 = (bf16[8,128,128]{2,1,0:T(8,128)(2,1)S(1)}, bf16[8,128,128]{2,1,0:T(8,128)(2,1)S(1)}, u32[]{:S(2)}, u32[]{:S(2)}) collective-permute-start(bf16[8,128,128]{2,1,0:T(8,128)(2,1)S(1)} %get-tuple-element.8), channel_id=1, source_target_pairs={{0,1},{1,2},{2,3},{3,4},{4,5},{5,6},{6,7},{7,8},{8,9},{9,10},{10,1... | collective-permute-start | bytes 786440 | tf_op jit(solution)/shard_map/ppermute | solution.py:26
  14.8 22.0 %collective-permute-start.3 = (bf16[8,128,128]{2,1,0:T(8,128)(2,1)S(1)}, bf16[8,128,128]{2,1,0:T(8,128)(2,1)S(1)}, u32[]{:S(2)}, u32[]{:S(2)}) collective-permute-start(bf16[8,128,128]{2,1,0:T(8,128)(2,1)S(1)} %get-tuple-element.6), channel_id=1, source_target_pairs={{0,63},{1,0},{2,1},{3,2},{4,3},{5,4},{6,5},{7,6},{8,7},{9,8},{10,9... | collective-permute-start | bytes 786440 | tf_op jit(solution)/shard_map/ppermute | solution.py:26
  21.3 15.8 %collective-permute-start.4 = (bf16[8,128,128]{2,1,0:T(8,128)(2,1)S(1)}, bf16[8,128,128]{2,1,0:T(8,128)(2,1)S(1)}, u32[]{:S(2)}, u32[]{:S(2)}) collective-permute-start(bf16[8,128,128]{2,1,0:T(8,128)(2,1)S(1)} %get-tuple-element.5), channel_id=1, source_target_pairs={{0,62},{1,63},{2,0},{3,1},{4,2},{5,3},{6,4},{7,5},{8,6},{9,7},{10,... | collective-permute-start | bytes 786440 | tf_op jit(solution)/shard_map/ppermute | solution.py:26
  50.7 1.0 copy-start
Sparse Core Ops, SparseCore 0:
  54.4 123.5 all-reduce.1
where the time goes:
time: 212 us; the launch traced here: 211 us
  waiting for transfers between devices  137 us (65%)
  other arithmetic  24.9 us (12%)
  between operations  13.6 us (6%)
  matrix products  13.1 us (6%)
  starting transfers between devices  11.8 us (6%)
  local copies, waits for them, and re-layouts  10.6 us (5%)
    psum x1, waiting for transfers between devices, body(): summed = lax.psum(partial_value, 'shard')  122 us
    ppermute x4, waiting for transfers between devices, from_behind(): lax.ppermute(x, axis, [(i, (i + by) % length) for i in range(length)])  14.8 us
    another operation x3, other arithmetic, body(): factor = jnp.linalg.cholesky(gram_matrix)  12.4 us
    ppermute x4, starting transfers between devices, from_behind(): lax.ppermute(x, axis, [(i, (i + by) % length) for i in range(length)])  11.8 us
    another operation x2, other arithmetic, body(): result = jax.scipy.linalg.solve_triangular(factor, update.T, lower=True).T  10.5 us
    dot_general x1, matrix products, body(): jnp.einsum('jab,jbr->jar', tile_grid, fetched, preferred_element_type=jnp...  7.6 us
  transfers between devices with their start and end apart: 6, of which 5 were waited for; matrix products, arithmetic and copies ran while one was open for 2% of the time, Pallas kernels for 0%

commit v1 on v0

--- a/solution.py
+++ b/solution.py
@@ -1,3 +1,4 @@
+import functools
 import jax
 import jax.numpy as jnp
 from jax import lax
@@ -9,6 +10,13 @@
 HALF = 2
 PAIRS = 5
 EPSILON = 1e-05
+
+
+def _find_loops(slab_in, device_axis):
+    return jnp.sum(lax.all_gather(slab_in, device_axis), axis=0)
+
+
+see_halves = functools.partial(_find_loops, device_axis="shard")
 
 
 def from_partner(block, axis, stride):
@@ -69,7 +77,7 @@
         precision=lax.Precision.HIGHEST,
     ).reshape(block_rows * TB, RANK)
     partial_value = jnp.einsum("nr,ns->rs", update, update, precision=lax.Precision.HIGHEST)
-    summed = lax.psum(partial_value, "shard")
+    summed = see_halves(partial_value)
     owners = lax.axis_size("shard")
     gram_matrix = summed / (update.shape[0] * owners) + EPSILON * jnp.eye(RANK, dtype=jnp.float32)
     factor = jnp.linalg.cholesky(gram_matrix)

time: 212 us -> 158 us (0.75)
  waiting for transfers between devices: 137 us -> 82.6 us
    psum x1 -> x0, waiting for transfers between devices: 122 us -> none  [body(): summed = lax.psum(partial_value, 'shard')]
    all_gather x0 -> x1, waiting for transfers between devices: none -> 66.4 us  [_find_loops(): return jnp.sum(lax.all_gather(slab_in, device_axis), axis=0)]
    reduce_sum x0 -> x1, other arithmetic: none -> 2.41 us  [_find_loops(): return jnp.sum(lax.all_gather(slab_in, device_axis), axis=0)]
  transfers between devices with their start and end apart: 6 -> 6, of which waited for: 5 -> 6; matrix products, arithmetic and copies ran while one was open for 2% -> 2% of each run, Pallas kernels for 0% -> 0%
where the time goes in v1:
time: 158 us
  waiting for transfers between devices  82.6 us (52%)
  other arithmetic  25.6 us (16%)
  between operations  13.6 us (9%)
  matrix products  13.2 us (8%)
  starting transfers between devices  11.8 us (7%)
  local copies, waits for them, and re-layouts  10.7 us (7%)
    all_gather x1, waiting for transfers between devices, _find_loops(): return jnp.sum(lax.all_gather(slab_in, device_axis), axis=0)  66.4 us
    ppermute x4, waiting for transfers between devices, from_behind(): lax.ppermute(x, axis, [(i, (i + by) % length) for i in range(length)])  15.8 us
    another operation x3, other arithmetic, body(): factor = jnp.linalg.cholesky(gram_matrix)  12.4 us
    ppermute x4, starting transfers between devices, from_behind(): lax.ppermute(x, axis, [(i, (i + by) % length) for i in range(length)])  11.8 us
    another operation x2, other arithmetic, body(): result = jax.scipy.linalg.solve_triangular(factor, update.T, lower=True).T  10.5 us
    dot_general x1, matrix products, body(): jnp.einsum('jab,jbr->jar', tile_grid, fetched, preferred_element_type=jnp...  7.6 us
  transfers between devices with their start and end apart: 6, of which 6 were waited for; matrix products, arithmetic and copies ran while one was open for 2% of the time, Pallas kernels for 0%

profile of v1, /device:TPU:0, one launch (start us, length us, event | category | flops | bytes accessed | tf_op | source)
XLA Modules:
  0.0 157.5 jit_solution(16970037014163914192)
XLA Ops:
  6.5 0.8 reshape.109
  7.4 0.8 fusion.10
  8.7 0.8 gather_fusion
  9.8 8.7 %collective-permute-start.4 = (bf16[8,128,128]{2,1,0:T(8,128)(2,1)S(1)}, bf16[8,128,128]{2,1,0:T(8,128)(2,1)S(1)}, u32[]{:S(2)}, u32[]{:S(2)}) collective-permute-start(bf16[8,128,128]{2,1,0:T(8,128)(2,1)S(1)} %get-tuple-element.5), channel_id=1, source_target_pairs={{0,62},{1,63},{2,0},{3,1},{4,2},{5,3},{6,4},{7,5},{8,6},{9,7},{10,... | collective-permute-start | bytes 786440 | tf_op jit(solution)/shard_map/ppermute | solution.py:34
  18.5 0.7 collective-permute-start.3
  19.2 1.3 collective-permute-start.2
  20.5 1.1 collective-permute-start.1
  21.8 3.4 %collective-permute-done.4 = bf16[8,128,128]{2,1,0:T(8,128)(2,1)S(1)} collective-permute-done((bf16[8,128,128]{2,1,0:T(8,128)(2,1)S(1)}, bf16[8,128,128]{2,1,0:T(8,128)(2,1)S(1)}, u32[]{:S(2)}, u32[]{:S(2)}) %collective-permute-start.4) | collective-permute-done | bytes 262176 | tf_op jit(solution)/shard_map/ppermute | solution.py:34
  25.3 5.1 %collective-permute-done.3 = bf16[8,128,128]{2,1,0:T(8,128)(2,1)S(1)} collective-permute-done((bf16[8,128,128]{2,1,0:T(8,128)(2,1)S(1)}, bf16[8,128,128]{2,1,0:T(8,128)(2,1)S(1)}, u32[]{:S(2)}, u32[]{:S(2)}) %collective-permute-start.3) | collective-permute-done | bytes 262176 | tf_op jit(solution)/shard_map/ppermute | solution.py:34
  30.5 6.3 %collective-permute-done.2 = bf16[8,128,128]{2,1,0:T(8,128)(2,1)S(1)} collective-permute-done((bf16[8,128,128]{2,1,0:T(8,128)(2,1)S(1)}, bf16[8,128,128]{2,1,0:T(8,128)(2,1)S(1)}, u32[]{:S(2)}, u32[]{:S(2)}) %collective-permute-start.2) | collective-permute-done | bytes 262176 | tf_op jit(solution)/shard_map/ppermute | solution.py:34
  37.0 1.0 collective-permute-done.1
  38.3 7.6 %fusion.12 = f32[5,128,1024]{2,1,0:T(8,128)S(1)} fusion(bf16[5,1024,128]{1,2,0:T(8,128)(2,1)S(1)} %constant_dynamic-update-slice_fusion, bf16[5,1024,1024]{2,1,0:T(8,128)(2,1)} %bitcast.58), kind=kOutput, calls=%fused_computation.42 | convolution fusion | flops 1342177280 | bytes 14417920 | tf_op jit(solution)/shard_map/jab,jbr->jar/dot_general | solution.py:66
  45.9 2.1 %copy.34 = f32[80,8,8,128]{3,2,1,0:T(8,128)} copy(f32[80,8,8,128]{3,1,2,0:T(8,128)S(1)} %bitcast.59) | data formatting | bytes 5242880
  48.0 2.6 %copy.24 = f32[5,8,128,128]{3,1,0,2:T(8,128)S(1)} copy(f32[5,8,128,128]{2,1,3,0:T(8,128)} %bitcast.60) | data formatting | bytes 5242880 | tf_op jit(solution)/shard_map/reshape | solution.py:76
  50.6 1.1 convolution_bitcast_fusion.1
  51.7 1.0 copy-done
  52.7 2.5 %convolution_bitcast_fusion.2 = f32[128,128]{1,0:T(8,128)} fusion(f32[16,128,128]{2,0,1:T(8,128)S(1)} %convolution_bitcast_fusion.1), kind=kOutput, calls=%fused_computation.4 | convolution fusion | flops 402653184 | bytes 1114112 | tf_op jit(solution)/shard_map/nr,ns->rs/dot_general | solution.py:79
  55.2 1.6 copy.25
  56.8 66.4 %all-gather.3.cloned.1.call-done = f32[8192,128]{1,0:T(8,128)} async-done(((f32[128,128]{1,0:T(8,128)}), f32[8192,128]{1,0:T(8,128)}) %all-gather.3.cloned.1.call-update) | async-done | bytes 4194320 | tf_op jit(solution)/shard_map/all_gather | solution.py:16
  123.2 2.4 %reduce_sum.9 = f32[128,128]{1,0:T(8,128)S(1)} reduce(f32[64,128,128]{2,1,0:T(8,128)} %bitcast.62, f32[]{:T(128)} %constant.73.clone.1), dimensions={0}, to_apply=%region_0.1 | reduce | flops 1032192 | bytes 4259844 | tf_op jit(solution)/shard_map/reduce_sum | solution.py:16
  125.9 11.7 %cholesky.16 = f32[128,128]{1,0:T(8,128)S(1)} custom-call(f32[128,128]{1,0:T(8,128)S(1)} %fusion.3), custom_call_target="Cholesky" | custom-call | tf_op jit(solution)/shard_map/jit(cholesky)/cholesky | solution.py:83
  138.2 0.7 fusion
  138.9 9.8 %custom-call.7 = f32[1,128,128]{1,2,0:T(8,128)S(1)} custom-call(f32[1,128,128]{2,1,0:T(8,128)S(1)} %fusion), custom_call_target="InvertDiagBlocksLowerTriangular" | custom-call | tf_op jit(solution)/shard_map/jit(_solve_triangular)/triangular_solve | solution.py:84
  148.7 1.9 %convolution_bitcast_fusion = f32[1,2048,128]{2,1,0:T(8,128)} fusion(f32[2048,128]{1,0:T(8,128)S(1)} %bitcast.63, f32[1,128,128]{1,2,0:T(8,128)S(1)} %custom-call.7), kind=kOutput, calls=%fused_computation.1 | convolution fusion | flops 402653184 | bytes 2162688 | tf_op jit(solution)/shard_map/jit(_solve_triangular)/triangular_solve | solution.py:84
  (29 shorter events, 2.7 us)
Async XLA Ops:
  6.5 116.7 %all-gather.3.cloned.1.call-start = ((), (), s32[]{:S(2)}) async-start(), calls=%async_computation | async-start | bytes 4259840 | tf_op jit(solution)/shard_map/all_gather | solution.py:16
  6.5 2.1 %collective-permute-start = (bf16[16,128,128]{2,1,0:T(8,128)(2,1)}, bf16[16,128,128]{2,1,0:T(8,128)(2,1)S(1)}, u32[]{:S(2)}, u32[]{:S(2)}) collective-permute-start(bf16[16,128,128]{2,1,0:T(8,128)(2,1)} %bitcast.69), channel_id=1, source_target_pairs={{0,64},{64,0},{1,65},{65,1},{2,66},{66,2},{3,67},{67,3},{4,68},{68... | collective-permute-start | bytes 1572872 | tf_op jit(solution)/shard_map/ppermute | solution.py:29
  9.8 15.4 %collective-permute-start.4 = (bf16[8,128,128]{2,1,0:T(8,128)(2,1)S(1)}, bf16[8,128,128]{2,1,0:T(8,128)(2,1)S(1)}, u32[]{:S(2)}, u32[]{:S(2)}) collective-permute-start(bf16[8,128,128]{2,1,0:T(8,128)(2,1)S(1)} %get-tuple-element.5), channel_id=1, source_target_pairs={{0,62},{1,63},{2,0},{3,1},{4,2},{5,3},{6,4},{7,5},{8,6},{9,7},{10,... | collective-permute-start | bytes 786440 | tf_op jit(solution)/shard_map/ppermute | solution.py:34
  18.5 11.9 %collective-permute-start.3 = (bf16[8,128,128]{2,1,0:T(8,128)(2,1)S(1)}, bf16[8,128,128]{2,1,0:T(8,128)(2,1)S(1)}, u32[]{:S(2)}, u32[]{:S(2)}) collective-permute-start(bf16[8,128,128]{2,1,0:T(8,128)(2,1)S(1)} %get-tuple-element.6), channel_id=1, source_target_pairs={{0,63},{1,0},{2,1},{3,2},{4,3},{5,4},{6,5},{7,6},{8,7},{9,8},{10,9... | collective-permute-start | bytes 786440 | tf_op jit(solution)/shard_map/ppermute | solution.py:34
  19.2 17.7 %collective-permute-start.2 = (bf16[8,128,128]{2,1,0:T(8,128)(2,1)S(1)}, bf16[8,128,128]{2,1,0:T(8,128)(2,1)S(1)}, u32[]{:S(2)}, u32[]{:S(2)}) collective-permute-start(bf16[8,128,128]{2,1,0:T(8,128)(2,1)S(1)} %get-tuple-element.8), channel_id=1, source_target_pairs={{0,1},{1,2},{2,3},{3,4},{4,5},{5,6},{6,7},{7,8},{8,9},{9,10},{10,1... | collective-permute-start | bytes 786440 | tf_op jit(solution)/shard_map/ppermute | solution.py:34
  20.5 17.5 %collective-permute-start.1 = (bf16[8,128,128]{2,1,0:T(8,128)(2,1)S(1)}, bf16[8,128,128]{2,1,0:T(8,128)(2,1)S(1)}, u32[]{:S(2)}, u32[]{:S(2)}) collective-permute-start(bf16[8,128,128]{2,1,0:T(8,128)(2,1)S(1)} %get-tuple-element.9), channel_id=1, source_target_pairs={{0,2},{1,3},{2,4},{3,5},{4,6},{5,7},{6,8},{7,9},{8,10},{9,11},{10,... | collective-permute-start | bytes 786440 | tf_op jit(solution)/shard_map/ppermute | solution.py:34
  51.7 1.0 copy-start
Sparse Core Ops, SparseCore 0:
  55.3 67.8 all-gather.2
